TPU v7x, 256 devices: a whole 4x4x8 slice. The times are simulated.
256 devices in a mesh: dp: 32 (over z_lo, y, x), tensor: 8 (over z_hi, core).
Axes of the slice: x: 4, y: 4, z: 8 (z_hi: 4, z_lo: 2; z = z_hi * 2 + z_lo), core: 2. Of those that a mesh axis runs over, the one named last changes fastest.
Arguments:
- rollout_rows: bfloat16 [16384, 4608], P(('dp', 'tensor')), may hold values from -6 to 6
- pack_dest: int32 [16384], P(('dp', 'tensor')), may hold values from 0 to 16383, as said below
- lengths: int32 [17], replicated, may hold values from 128 to 1536, as said below
- pattern: int32 [128, 128], P('dp'), may hold values from 0 to 1, as said below
- norm_gain: float32 [4608], replicated, may hold values from 0.1 to 1.9
- w_query: bfloat16 [4608, 2048], P(None, 'tensor'), may hold values from -0.1875 to 0.1875
- w_key: bfloat16 [4608, 1024], P(None, 'tensor'), may hold values from -0.1875 to 0.1875
- w_value: bfloat16 [4608, 1024], P(None, 'tensor'), may hold values from -0.09375 to 0.09375
- w_out: bfloat16 [2048, 4608], P('tensor'), may hold values from -0.125 to 0.125
- post_gain: float32 [4608], replicated, may hold values from 0.1 to 1.9
Outputs:
- layer_out: bfloat16 [16384, 4608], P(('dp', 'tensor'))
Inputs may be any that keep to these rules, and one draw needn't show every extreme that they name: `pack_dest`: a permutation of the pack rows; a rollout row goes to a pack row of the same tensor index, and the 64 rollout rows of one device go to each dp index exactly 2 at a time. `lengths`: all multiples of 128, summing to 16384; the prompt is shorter than 512. pattern[q, q] = 1; pattern[q, k] = 1 only where k <= q and key block k lies in the first 512 pack rows or in a dp shard at most 3 before query block q's shard.
All inputs are finite; a program needn't handle non-finite values.
Results may differ from a plain program's by a relative error of at most 0.017.
Values may be sent and summed in bfloat16 or wider, within the bound.
No kernel may reach another device: no remote copies, remote signals or barrier semaphores. Data moves between devices by JAX's collectives and lax.ppermute only.
A program may use at most 128 MiB of HBM per device.

v0:
```python
import jax
import jax.numpy as jnp
from jax import lax
from jax.sharding import PartitionSpec as P

HD = 128
BLK = 128
SOFT_CAP = 50.0
QUERY_SCALE = 1.0 / 12.0
ROPE_BASE = 10000.0
EPSILON = 1e-06


def positions(row_ids, lengths):
    bounds = jnp.cumsum(lengths)
    prompt = lengths[0]
    passed = (row_ids[:, None] >= bounds[None, :]).astype(jnp.int32)
    offset_start = jnp.sum(passed * lengths[None, :], axis=1)
    return jnp.where(row_ids < prompt, row_ids, prompt + row_ids - offset_start)


def rotate(values, angle_pos):
    half_width = values.shape[-1] // 2
    inverse_freq = jnp.power(
        ROPE_BASE, -(jnp.arange(half_width, dtype=jnp.float32) * 2.0) / values.shape[-1]
    )
    angles = angle_pos[:, None] * inverse_freq[None, :]
    cosine = jnp.cos(angles)[:, None, :]
    sine_part = jnp.sin(angles)[:, None, :]
    front_half = values[..., :half_width]
    back_half = values[..., half_width:]
    return jnp.concatenate(
        [front_half * cosine - back_half * sine_part, back_half * cosine + front_half * sine_part],
        axis=-1,
    )


def rms_scale(values, gain):
    return values * lax.rsqrt(jnp.mean(values * values, axis=-1, keepdims=True) + EPSILON) * gain


def attend(running, queries, key_value, pats, q_start, low_block, high_block):
    query_count = queries.shape[0]
    head_count = queries.shape[1]
    head_width = queries.shape[3]
    block_count = key_value.shape[0] // BLK
    key_blocks = key_value.reshape(block_count, BLK, 2, head_count, head_width)
    q_ids = q_start + jnp.arange(query_count, dtype=jnp.int32)

    def step(block_index, current):
        column = lax.dynamic_index_in_dim(
            pats, jnp.clip(block_index, 0, pats.shape[1] - 1), 1, keepdims=False
        )
        active = (block_index >= low_block) & (block_index < high_block) & jnp.any(column == 1)

        def compute(inner):
            weighted, totals = inner
            block_pair = lax.dynamic_index_in_dim(key_blocks, block_index, 0, keepdims=False)
            scores = (
                jnp.einsum(
                    "qhgd,khd->hgqk", queries, block_pair[:, 0], preferred_element_type=jnp.float32
                )
                * QUERY_SCALE
            )
            capped = SOFT_CAP * jnp.tanh(scores / SOFT_CAP)
            k_ids = block_index * BLK + jnp.arange(BLK, dtype=jnp.int32)
            allowed = (jnp.repeat(column, BLK) == 1)[:, None] & (k_ids[None, :] <= q_ids[:, None])
            weights = jnp.where(allowed, jnp.exp(capped), jnp.float32(0.0))
            rounded = weights.astype(jnp.bfloat16)
            weighted = weighted + jnp.einsum(
                "hgqk,khd->hgqd", rounded, block_pair[:, 1], preferred_element_type=jnp.float32
            )
            totals = totals + jnp.sum(weights, axis=-1)
            return (weighted, totals)

        return lax.cond(active, compute, lambda inner: inner, current)

    return lax.fori_loop(0, block_count, step, running)


def body(
    rollout_rows, pack_dest, lengths, pattern, norm_gain, w_query, w_key, w_value, w_out, post_gain
):
    tok_count = rollout_rows.shape[0]
    data_count = lax.axis_size("dp")
    tens_count = lax.axis_size("tensor")
    shard_len = tok_count * tens_count
    per_peer = tok_count // data_count
    target_dev = pack_dest // shard_len
    target_slot = pack_dest % tok_count
    order_ids = jnp.arange(tok_count, dtype=jnp.int32)
    before = (target_dev[:, None] == target_dev[None, :]) & (
        order_ids[None, :] < order_ids[:, None]
    )
    bucket_rank = jnp.sum(before.astype(jnp.int32), axis=1)
    send_pos = target_dev * per_peer + bucket_rank
    placer = order_ids[:, None] == send_pos[None, :]
    send_rows = jnp.dot(
        placer.astype(jnp.bfloat16), rollout_rows, preferred_element_type=jnp.float32
    ).astype(jnp.bfloat16)
    send_slots = jnp.sum(jnp.where(placer, target_slot[None, :], 0), axis=1)
    got_rows, got_slots = (
        lax.all_to_all(
            send_rows.reshape(data_count, per_peer, -1),
            "dp",
            split_axis=0,
            concat_axis=0,
            tiled=True,
        ),
        lax.all_to_all(
            send_slots.reshape(data_count, per_peer), "dp", split_axis=0, concat_axis=0, tiled=True
        ),
    )
    arrange = order_ids[:, None] == got_slots.reshape(tok_count)[None, :]
    packed = jnp.dot(
        arrange.astype(jnp.bfloat16),
        got_rows.reshape(tok_count, -1),
        preferred_element_type=jnp.float32,
    ).astype(jnp.bfloat16)
    normed = rms_scale(packed.astype(jnp.float32), norm_gain).astype(jnp.bfloat16)
    data_index = lax.axis_index("dp")
    base_row = data_index * shard_len
    query_cols = w_query.shape[1]
    pair_cols = w_key.shape[1]
    kv_heads = pair_cols // HD
    group_size = query_cols // HD // kv_heads
    portion = lax.all_gather(normed, "tensor", axis=0, tiled=True)
    row_ids = base_row + jnp.arange(portion.shape[0], dtype=jnp.int32)
    angle_pos = positions(row_ids, lengths).astype(jnp.float32)
    query_part = jnp.dot(portion, w_query, preferred_element_type=jnp.float32)
    key_part = jnp.dot(portion, w_key, preferred_element_type=jnp.float32)
    value_part = jnp.dot(portion, w_value, preferred_element_type=jnp.float32)
    query_part = rotate(query_part.reshape(-1, query_cols // HD, HD), angle_pos).reshape(
        -1, query_cols
    )
    key_part = rotate(key_part.reshape(-1, kv_heads, HD), angle_pos).reshape(-1, pair_cols)
    projected = jnp.concatenate([query_part, key_part, value_part], axis=1).astype(jnp.bfloat16)
    queries = projected[:, :query_cols].reshape(shard_len, kv_heads, group_size, HD)
    key_value = projected[:, query_cols:]
    block_total = pattern.shape[1]
    start_state = (
        jnp.zeros((kv_heads, group_size, shard_len, HD), jnp.float32),
        jnp.zeros((kv_heads, group_size, shard_len), jnp.float32),
    )
    weighted, totals = attend(
        start_state,
        queries,
        lax.all_gather(key_value, "dp", axis=0, tiled=True),
        pattern,
        base_row,
        0,
        block_total,
    )
    attended = weighted / totals[..., None]
    heads_out = (
        jnp.transpose(attended, (2, 0, 1, 3)).reshape(shard_len, query_cols).astype(jnp.bfloat16)
    )
    summed = lax.psum_scatter(
        jnp.dot(heads_out, w_out, preferred_element_type=jnp.float32).astype(jnp.bfloat16),
        "tensor",
        scatter_dimension=0,
        tiled=True,
    ).astype(jnp.float32)
    result = packed.astype(jnp.float32) + rms_scale(summed, post_gain)
    return result.astype(jnp.bfloat16)


def solution(mesh):
    placed = (
        P(("dp", "tensor"), None),
        P(("dp", "tensor")),
        P(),
        P("dp", None),
        P(),
        P(None, "tensor"),
        P(None, "tensor"),
        P(None, "tensor"),
        P("tensor", None),
        P(),
    )
    return jax.shard_map(
        body, mesh=mesh, in_specs=placed, out_specs=P(("dp", "tensor"), None), check_vma=False
    )
```

profile of v0, /device:TPU:65, one launch (start us, length us, event | category | flops | bytes accessed | tf_op | source)
XLA Modules:
  0.0 567.5 jit_solution(9726202630693829458)
XLA Ops:
  6.5 0.8 and_select_fusion
  8.4 8.4 %all-to-all-start = ((s32[32,1,2]{2,1,0:T(1,128)}), s32[32,1,2]{2,1,0:T(1,128)S(1)}, u32[]{:S(2)}, u32[]{:S(2)}) async-start(s32[32,1,2]{2,1,0:T(1,128)} %bitcast.12), calls=%async_computation | async-start | bytes 32768 | tf_op jit(solution)/shard_map/all_to_all | solution.py:110
  16.8 1.4 convolution_convert_fusion.2
  18.1 1.0 reshape.231
  19.2 4.6 all-to-all-done
  23.7 3.9 all-to-all-start.1
  29.0 8.0 %all-to-all-done.1 = bf16[32,2,4608]{2,1,0:T(2,128)(2,1)S(1)} async-done(((bf16[32,2,4608]{2,1,0:T(2,128)(2,1)}), bf16[32,2,4608]{2,1,0:T(2,128)(2,1)S(1)}, u32[]{:S(2)}, u32[]{:S(2)}) %all-to-all-start.1) | async-done | bytes 589856 | tf_op jit(solution)/shard_map/all_to_all | solution.py:103
  37.7 1.0 copy-done.2
  38.7 1.0 multiply_convert_fusion
  42.6 55.9 %all-gather.3.cloned.1.call-done = bf16[512,4608]{1,0:T(8,128)(2,1)} async-done(((bf16[64,4608]{1,0:T(8,128)(2,1)}), bf16[512,4608]{1,0:T(8,128)(2,1)}) %all-gather.3.cloned.1.call-update) | async-done | bytes 4718608 | tf_op jit(solution)/shard_map/all_gather | solution.py:127
  98.5 4.2 convolution_bitcast_fusion.1
  103.3 1.7 convolution_convert_fusion.3
  106.1 1.8 multiply_cosine_fusion
  107.9 4.5 fusion.30
  113.4 1.2 copy.42
  114.5 1.2 subtract_convert_fusion
  115.9 138.8 %all-gather.5.cloned.1.call-done = bf16[16384,256]{0,1:T(8,128)(2,1)} async-done(((bf16[512,256]{0,1:T(8,128)(2,1)}), bf16[16384,256]{0,1:T(8,128)(2,1)}) %all-gather.5.cloned.1.call-update) | async-done | bytes 8388624 | tf_op jit(solution)/shard_map/all_gather | solution.py:148
  254.7 9.2 %copy.43 = bf16[32,8,128,128]{3,2,1,0:T(8,128)(2,1)} copy(bf16[32,8,128,128]{3,1,2,0:T(8,128)(2,1)} %bitcast.70) | data formatting | bytes 16777216
  263.9 13.1 %copy.38 = bf16[128,128,2,1,128]{4,1,2,3,0:T(8,128)(2,1)} copy(bf16[128,128,2,1,128]{1,0,4,2,3:T(8,128)(2,1)} %bitcast.69) | data formatting | bytes 16777216
  277.0 178.3 %while.16 = (s32[]{:T(128)}, f32[1,2,512,128]{3,2,1,0:T(8,128)S(1)}, f32[1,2,512]{2,1,0:T(2,128)S(1)}, s32[4,128]{0,1:T(8,128)S(1)}, bf16[128,128,2,1,128]{4,1,2...) while((s32[]{:T(128)}, ...), condition=%wide.region_10.11_spmd.clone, body=%wide.region_5.10_spmd.clone.sunk | while | flops 68027032 | bytes 2189677 | solution.py:78
  278.3 1.7 conditional.3
  278.3 0.8 dynamic-slice_bitcast_fusion
  281.4 1.7 conditional.3
  281.4 0.8 dynamic-slice_bitcast_fusion
  284.4 1.7 conditional.3
  284.4 0.8 dynamic-slice_bitcast_fusion
  287.5 1.7 conditional.3
  287.5 0.8 dynamic-slice_bitcast_fusion
  455.5 3.5 convolution_convert_fusion
  459.1 98.5 %reduce-scatter.2.cloned.1.call-done = bf16[64,4608]{1,0:T(8,128)(2,1)} async-done(((bf16[512,4608]{1,0:T(8,128)(2,1)}), bf16[64,4608]{1,0:T(8,128)(2,1)}) %reduce-scatter.2.cloned.1.call-update) | async-done | bytes 589840 | tf_op jit(solution)/shard_map/reduce_scatter | solution.py:158
  557.6 1.3 fusion.12
  558.9 2.1 fusion.15
  (464 shorter events, 96.2 us)
Async XLA Ops:
  6.5 449.0 %copy-start = (bf16[256,4608]{1,0:T(8,128)(2,1)S(1)}, bf16[256,4608]{1,0:T(8,128)(2,1)}, u32[]{:S(2)}) copy-start(bf16[256,4608]{1,0:T(8,128)(2,1)} %param.22) | copy-start | bytes 7077892
  8.4 15.4 %all-to-all-start = ((s32[32,1,2]{2,1,0:T(1,128)}), s32[32,1,2]{2,1,0:T(1,128)S(1)}, u32[]{:S(2)}, u32[]{:S(2)}) async-start(s32[32,1,2]{2,1,0:T(1,128)} %bitcast.12), calls=%async_computation | async-start | bytes 32768 | tf_op jit(solution)/shard_map/all_to_all | solution.py:110
  23.7 13.3 %all-to-all-start.1 = ((bf16[32,2,4608]{2,1,0:T(2,128)(2,1)}), bf16[32,2,4608]{2,1,0:T(2,128)(2,1)S(1)}, u32[]{:S(2)}, u32[]{:S(2)}) async-start(bf16[32,2,4608]{2,1,0:T(2,128)(2,1)} %reshape.231), calls=%async_computation.1 | async-start | bytes 1179648 | tf_op jit(solution)/shard_map/all_to_all | solution.py:103
  27.6 70.9 %all-gather.3.cloned.1.call-start = ((), (), s32[]{:S(2)}) async-start(), calls=%async_computation.3 | async-start | bytes 5308416 | tf_op jit(solution)/shard_map/all_gather | solution.py:127
  37.3 1.4 copy-start.6
  37.7 1.0 copy-start.2
  38.7 1.1 copy-start.7
  38.7 59.8 %copy-start.4 = (bf16[4608,128]{1,0:T(8,128)(2,1)S(1)}, bf16[4608,128]{1,0:T(8,128)(2,1)}, u32[]{:S(2)}) copy-start(bf16[4608,128]{1,0:T(8,128)(2,1)} %param.20) | copy-start | bytes 3538948
  39.7 215.0 %all-gather.5.cloned.1.call-start = ((), (), s32[]{:S(2)}) async-start(), calls=%async_computation.4 | async-start | bytes 8650752 | tf_op jit(solution)/shard_map/all_gather | solution.py:148
  98.5 4.8 copy-start.1
  98.5 4.8 copy-start.5
  103.3 2.7 copy-start.8
  105.7 451.9 %reduce-scatter.2.cloned.1.call-start = ((), (), s32[]{:S(2)}) async-start(), calls=%async_computation.5 | async-start | bytes 5308416 | tf_op jit(solution)/shard_map/reduce_scatter | solution.py:158
  459.1 99.8 %copy-start.3 = (f32[64,4608]{1,0:T(8,128)S(1)}, f32[64,4608]{1,0:T(8,128)}, u32[]{:S(2)}) copy-start(f32[64,4608]{1,0:T(8,128)} %copy-done.2) | copy-start | bytes 3538948
Sparse Core Ops, SparseCore 0:
  39.9 58.5 all-gather.2
  105.9 148.7 all-gather.4
  459.2 98.3 reduce-scatter.1
where the time goes:
time: 570 us; the launch traced here: 568 us
  waiting for transfers between devices  306 us (54%)
  other arithmetic  95.4 us (17%)
  loops' own time  89.2 us (16%)
  local copies, waits for them, and re-layouts  33 us (6%)
  matrix products  18.1 us (3%)
  between operations  13.4 us (2%)
  starting transfers between devices  12.6 us (2%)
    all_gather x1, waiting for transfers between devices, body(): lax.all_gather(key_value, 'dp', axis=0, tiled=True)  139 us
    reduce_scatter x1, waiting for transfers between devices, body(): lax.psum_scatter(jnp.dot(heads_out, w_out, preferred_element_type=jnp.flo...  98.5 us
    another operation x1, loops' own time, attend(): return lax.fori_loop(0, block_count, step, running)  87.4 us
    reduce_or x128, other arithmetic, step(): jnp.any(column == 1)  82.1 us
    all_gather x1, waiting for transfers between devices, body(): portion = lax.all_gather(normed, 'tensor', axis=0, tiled=True)  55.9 us
    unnamed x23, local copies, waits for them, and re-layouts  24.8 us
  transfers between devices with their start and end apart: 5, of which 5 were waited for; matrix products, arithmetic and copies ran while one was open for 3% of the time, Pallas kernels for 0%

commit v1 on v0

--- a/solution.py
+++ b/solution.py
@@ -145,7 +145,9 @@
     weighted, totals = attend(
         start_state,
         queries,
-        lax.all_gather(key_value, "dp", axis=0, tiled=True),
+        jnp.concatenate(
+            lax.all_to_all(jnp.stack([key_value] * lax.axis_size("dp")), "dp", 0, 0), axis=0
+        ),
         pattern,
         base_row,
         0,

time: 570 us -> 560 us (0.982)
  waiting for transfers between devices: 306 us -> 267 us
  local copies, waits for them, and re-layouts: 33 us -> 53.3 us
  starting transfers between devices: 12.6 us -> 19.6 us
    all_gather x1 -> x0, waiting for transfers between devices: 139 us -> none  [body(): lax.all_gather(key_value, 'dp', axis=0, tiled=True)]
    all_to_all x0 -> x1, waiting for transfers between devices: none -> 118 us  [body(): lax.all_to_all(jnp.stack([key_value] * lax.axis_size('dp')), 'dp', 0, 0)]
    another operation x1 -> x3, local copies, waits for them, and re-layouts: 0.68 us -> 18.7 us  [the longest x1 13.9 us: attend(): key_blocks = key_value.reshape(block_count, BLK, 2, head_count, head_width)]
    reduce_scatter x1, waiting for transfers between devices: 98.5 us -> 80.7 us  [body(): lax.psum_scatter(jnp.dot(heads_out, w_out, preferred_element_type=jnp.flo...]
    all_to_all x0 -> x1, local copies, waits for them, and re-layouts: none -> 11.3 us  [body(): lax.all_to_all(jnp.stack([key_value] * lax.axis_size('dp')), 'dp', 0, 0)]
    unnamed x23 -> x20, local copies, waits for them, and re-layouts: 24.8 us -> 15.6 us
    all_to_all x0 -> x1, starting transfers between devices: none -> 7.07 us  [body(): lax.all_to_all(jnp.stack([key_value] * lax.axis_size('dp')), 'dp', 0, 0)]
where the time goes in v1:
time: 560 us; the launch traced here: 557 us
  waiting for transfers between devices  267 us (48%)
  other arithmetic  95.6 us (17%)
  loops' own time  89.2 us (16%)
  local copies, waits for them, and re-layouts  53.3 us (10%)
  starting transfers between devices  19.6 us (4%)
  matrix products  18.1 us (3%)
  between operations  13.7 us (2%)
    all_to_all x1, waiting for transfers between devices, body(): lax.all_to_all(jnp.stack([key_value] * lax.axis_size('dp')), 'dp', 0, 0)  118 us
    another operation x1, loops' own time, attend(): return lax.fori_loop(0, block_count, step, running)  87.3 us
    reduce_or x128, other arithmetic, step(): jnp.any(column == 1)  82.1 us
    reduce_scatter x1, waiting for transfers between devices, body(): lax.psum_scatter(jnp.dot(heads_out, w_out, preferred_element_type=jnp.flo...  80.7 us
    all_gather x1, waiting for transfers between devices, body(): portion = lax.all_gather(normed, 'tensor', axis=0, tiled=True)  55.6 us
    unnamed x20, local copies, waits for them, and re-layouts  15.6 us
    another operation x1, local copies, waits for them, and re-layouts, attend(): key_blocks = key_value.reshape(block_count, BLK, 2, head_count, head_width)  13.9 us
    all_to_all x1, local copies, waits for them, and re-layouts, body(): lax.all_to_all(jnp.stack([key_value] * lax.axis_size('dp')), 'dp', 0, 0)  11.3 us
  transfers between devices with their start and end apart: 5, of which 5 were waited for; matrix products, arithmetic and copies ran while one was open for 3% of the time, Pallas kernels for 0%

profile of v1, /device:TPU:65, one launch (start us, length us, event | category | flops | bytes accessed | tf_op | source)
XLA Modules:
  0.0 556.7 jit_solution(13762436295810427857)
XLA Ops:
  8.4 8.4 %all-to-all-start = ((s32[32,1,2]{2,1,0:T(1,128)}), s32[32,1,2]{2,1,0:T(1,128)S(1)}, u32[]{:S(2)}, u32[]{:S(2)}) async-start(s32[32,1,2]{2,1,0:T(1,128)} %bitcast.12), calls=%async_computation | async-start | bytes 32768 | tf_op jit(solution)/shard_map/all_to_all | solution.py:110
  16.8 1.4 convolution_convert_fusion.2
  18.1 1.0 reshape.230
  19.2 4.7 all-to-all-done
  23.9 3.9 all-to-all-start.1
  29.3 8.1 %all-to-all-done.1 = bf16[32,2,4608]{2,1,0:T(2,128)(2,1)S(1)} async-done(((bf16[32,2,4608]{2,1,0:T(2,128)(2,1)}), bf16[32,2,4608]{2,1,0:T(2,128)(2,1)S(1)}, u32[]{:S(2)}, u32[]{:S(2)}) %all-to-all-start.1) | async-done | bytes 589856 | tf_op jit(solution)/shard_map/all_to_all | solution.py:103
  38.1 1.1 copy-done.2
  39.2 1.7 multiply_convert_fusion
  43.9 55.6 %all-gather.2.cloned.1.call-done = bf16[512,4608]{1,0:T(8,128)(2,1)} async-done(((bf16[64,4608]{1,0:T(8,128)(2,1)}), bf16[512,4608]{1,0:T(8,128)(2,1)}) %all-gather.2.cloned.1.call-update) | async-done | bytes 4718608 | tf_op jit(solution)/shard_map/all_gather | solution.py:127
  99.5 4.2 convolution_bitcast_fusion.1
  104.2 1.7 convolution_convert_fusion.3
  106.0 4.2 stack.2
  110.1 7.1 %all-to-all-start.2 = ((bf16[32,512,256]{1,2,0:T(8,128)(2,1)}), bf16[32,512,256]{1,2,0:T(8,128)(2,1)}, u32[]{:S(2)}, u32[]{:S(2)}) async-start(bf16[32,512,256]{1,2,0:T(8,128)(2,1)} %stack.2), calls=%async_computation.2 | async-start | bytes 16777216 | tf_op jit(solution)/shard_map/all_to_all | solution.py:149
  117.6 1.8 multiply_cosine_fusion
  119.4 4.5 fusion.30
  124.9 1.1 copy.44
  126.0 1.2 subtract_convert_fusion
  127.4 118.0 %all-to-all-done.2 = bf16[32,512,256]{1,2,0:T(8,128)(2,1)} async-done(((bf16[32,512,256]{1,2,0:T(8,128)(2,1)}), bf16[32,512,256]{1,2,0:T(8,128)(2,1)}, u32[]{:S(2)}, u32[]{:S(2)}) %all-to-all-start.2) | async-done | bytes 8388640 | tf_op jit(solution)/shard_map/all_to_all | solution.py:149
  245.4 11.3 %copy.36 = bf16[32,512,256]{1,0,2:T(8,128)(2,1)} copy(bf16[32,512,256]{1,2,0:T(8,128)(2,1)} %all-to-all-done.2) | data formatting | bytes 16777216 | tf_op jit(solution)/shard_map/all_to_all | solution.py:149
  256.7 13.9 %reshape_reshape.3 = bf16[128,128,2,1,128]{1,0,4,2,3:T(8,128)(2,1)} reshape(bf16[32,512,256]{1,0,2:T(8,128)(2,1)} %copy.36) | data formatting | bytes 16777216 | tf_op jit(solution)/shard_map/reshape;reshape | solution.py:47
  270.6 13.1 %copy.40 = bf16[128,128,2,1,128]{4,1,2,3,0:T(8,128)(2,1)} copy(bf16[128,128,2,1,128]{1,0,4,2,3:T(8,128)(2,1)} %reshape_reshape.3) | data formatting | bytes 16777216
  283.7 178.2 %while.16 = (s32[]{:T(128)}, f32[1,2,512,128]{3,2,1,0:T(8,128)S(1)}, f32[1,2,512]{2,1,0:T(2,128)S(1)}, s32[4,128]{0,1:T(8,128)S(1)}, bf16[128,128,2,1,128]{4,1,2...) while((s32[]{:T(128)}, ...), condition=%wide.region_10.11_spmd.clone, body=%wide.region_5.10_spmd.clone.sunk | while | flops 68027032 | bytes 2189677 | solution.py:78
  285.0 1.7 conditional.3
  285.1 0.8 dynamic-slice_bitcast_fusion
  288.1 1.7 conditional.3
  288.1 0.8 dynamic-slice_bitcast_fusion
  291.2 1.7 conditional.3
  294.2 1.7 conditional.3
  462.2 3.5 convolution_convert_fusion
  465.8 80.7 %reduce-scatter.2.cloned.1.call-done = bf16[64,4608]{1,0:T(8,128)(2,1)} async-done(((bf16[512,4608]{1,0:T(8,128)(2,1)}), bf16[64,4608]{1,0:T(8,128)(2,1)}) %reduce-scatter.2.cloned.1.call-update) | async-done | bytes 589840 | tf_op jit(solution)/shard_map/reduce_scatter | solution.py:160
  546.5 1.3 fusion.12
  547.8 2.1 fusion.15
  (463 shorter events, 98.2 us)
Async XLA Ops:
  6.5 455.7 %copy-start = (bf16[256,4608]{1,0:T(8,128)(2,1)S(1)}, bf16[256,4608]{1,0:T(8,128)(2,1)}, u32[]{:S(2)}) copy-start(bf16[256,4608]{1,0:T(8,128)(2,1)} %param.22) | copy-start | bytes 7077892
  8.4 15.5 %all-to-all-start = ((s32[32,1,2]{2,1,0:T(1,128)}), s32[32,1,2]{2,1,0:T(1,128)S(1)}, u32[]{:S(2)}, u32[]{:S(2)}) async-start(s32[32,1,2]{2,1,0:T(1,128)} %bitcast.12), calls=%async_computation | async-start | bytes 32768 | tf_op jit(solution)/shard_map/all_to_all | solution.py:110
  23.9 13.5 %all-to-all-start.1 = ((bf16[32,2,4608]{2,1,0:T(2,128)(2,1)}), bf16[32,2,4608]{2,1,0:T(2,128)(2,1)S(1)}, u32[]{:S(2)}, u32[]{:S(2)}) async-start(bf16[32,2,4608]{2,1,0:T(2,128)(2,1)} %reshape.230), calls=%async_computation.1 | async-start | bytes 1179648 | tf_op jit(solution)/shard_map/all_to_all | solution.py:103
  27.8 71.7 %all-gather.2.cloned.1.call-start = ((), (), s32[]{:S(2)}) async-start(), calls=%async_computation.4 | async-start | bytes 5308416 | tf_op jit(solution)/shard_map/all_gather | solution.py:127
  37.6 3.3 copy-start.6
  38.0 1.1 copy-start.2
  38.1 61.4 %copy-start.4 = (bf16[4608,128]{1,0:T(8,128)(2,1)S(1)}, bf16[4608,128]{1,0:T(8,128)(2,1)}, u32[]{:S(2)}) copy-start(bf16[4608,128]{1,0:T(8,128)(2,1)} %param.20) | copy-start | bytes 3538948
  99.5 4.8 copy-start.1
  99.5 4.8 copy-start.5
  110.1 7.3 %copy-start.7 = (s32[4,128]{1,0:T(4,128)S(1)}, s32[4,128]{1,0:T(4,128)}, u32[]{:S(2)}) copy-start(s32[4,128]{1,0:T(4,128)} %param.17) | copy-start | bytes 6148
  110.1 135.3 %all-to-all-start.2 = ((bf16[32,512,256]{1,2,0:T(8,128)(2,1)}), bf16[32,512,256]{1,2,0:T(8,128)(2,1)}, u32[]{:S(2)}, u32[]{:S(2)}) async-start(bf16[32,512,256]{1,2,0:T(8,128)(2,1)} %stack.2), calls=%async_computation.2 | async-start | bytes 16777216 | tf_op jit(solution)/shard_map/all_to_all | solution.py:149
  117.2 429.3 %reduce-scatter.2.cloned.1.call-start = ((), (), s32[]{:S(2)}) async-start(), calls=%async_computation.5 | async-start | bytes 5308416 | tf_op jit(solution)/shard_map/reduce_scatter | solution.py:160
  465.7 82.0 %copy-start.3 = (f32[64,4608]{1,0:T(8,128)S(1)}, f32[64,4608]{1,0:T(8,128)}, u32[]{:S(2)}) copy-start(f32[64,4608]{1,0:T(8,128)} %copy-done.2) | copy-start | bytes 3538948
Sparse Core Ops, SparseCore 0:
  41.0 58.3 all-gather.1
  465.9 80.5 reduce-scatter.1
